TPU v7x, 32 devices: a whole 2x2x4 slice. The times are simulated.
32 devices in a mesh: replica: 8 (over z, core), shard: 4 (over y, x).
Axes of the slice: x: 2, y: 2, z: 4, core: 2. Of those that a mesh axis runs over, the one named last changes fastest.
Arguments:
- tokens: bfloat16 [64, 512, 768], P(('replica', 'shard')), may hold values from -8 to 8
- lengths: int32 [64], P(('replica', 'shard')), may hold values from 256 to 512, as said below
- w_query: bfloat16 [768, 768], P('shard'), may hold values from -0.21875 to 0.21875
- b_query: bfloat16 [768], P('shard'), may hold values from -3 to 3
- w_key: bfloat16 [768, 768], P('shard'), may hold values from -0.21875 to 0.21875
- w_value: bfloat16 [768, 768], P('shard'), may hold values from -0.21875 to 0.21875
- b_value: bfloat16 [768], P('shard'), may hold values from -3 to 3
- w_attn_out: bfloat16 [768, 768], P('shard'), may hold values from -4 to 4
- b_attn_out: bfloat16 [768], P('shard'), may hold values from -3 to 3
- gain_one: bfloat16 [768], P('shard'), may hold values from 0.099609375 to 1.8984375
- shift_one: bfloat16 [768], P('shard'), may hold values from -2 to 2
- w_expand: bfloat16 [768, 3072], P('shard'), may hold values from -0.21875 to 0.21875
- b_expand: bfloat16 [3072], P('shard'), may hold values from -3 to 3
- w_contract: bfloat16 [3072, 768], P('shard'), may hold values from -0.109375 to 0.109375
- b_contract: bfloat16 [768], P('shard'), may hold values from -3 to 3
- gain_two: bfloat16 [768], P('shard'), may hold values from 0.099609375 to 1.8984375
- shift_two: bfloat16 [768], P('shard'), may hold values from -2 to 2
- w_colbert: bfloat16 [768, 128], P('shard'), may hold values from -0.21875 to 0.21875
- cotangent: bfloat16 [64, 512, 128], P(('replica', 'shard')), may hold values from -48 to 48
Outputs:
- embeddings: bfloat16 [64, 512, 128], P(('replica', 'shard'))
- grad_tokens: bfloat16 [64, 512, 768], P(('replica', 'shard'))
- grad_w_query: float32 [768, 768], P('shard')
- grad_b_query: float32 [768], P('shard')
- grad_w_key: float32 [768, 768], P('shard')
- grad_w_value: float32 [768, 768], P('shard')
- grad_b_value: float32 [768], P('shard')
- grad_w_attn_out: float32 [768, 768], P('shard')
- grad_b_attn_out: float32 [768], P('shard')
- grad_gain_one: float32 [768], P('shard')
- grad_shift_one: float32 [768], P('shard')
- grad_w_expand: float32 [768, 3072], P('shard')
- grad_b_expand: float32 [3072], P('shard')
- grad_w_contract: float32 [3072, 768], P('shard')
- grad_b_contract: float32 [768], P('shard')
- grad_gain_two: float32 [768], P('shard')
- grad_shift_two: float32 [768], P('shard')
- grad_w_colbert: float32 [768, 128], P('shard')
- rms_values: float32 [3], replicated
Inputs may be any that keep to these rules, and one draw needn't show every extreme that they name: `lengths`: valid leading positions of each sequence; some sequence has 512 of them and some has 256.
All inputs are finite; a program needn't handle non-finite values.
Results may differ from a plain program's by a relative error of at most 0.017.
Values may be sent and summed in bfloat16 or wider, within the bound.
No kernel may reach another device: no remote copies, remote signals or barrier semaphores. Data moves between devices by JAX's collectives and lax.ppermute only.
A program may use at most 256 MiB of HBM per device.

v0:
```python
from functools import partial

import jax
import jax.numpy as jnp
from jax import lax
from jax.sharding import PartitionSpec as P

HEADS = 12
HEAD_DIM = 64


norm_epsilon = 1e-12
masked_score = -1e30


def product(left, right):
    return jnp.dot(left, right, preferred_element_type=jnp.float32)


def product_left_t(left, right):
    return lax.dot_general(
        left, right, (((0,), (0,)), ((), ())), preferred_element_type=jnp.float32
    )


def product_right_t(left, right):
    return lax.dot_general(
        left, right, (((1,), (1,)), ((), ())), preferred_element_type=jnp.float32
    )


def layer_norm(summed, gain, shift):
    center = summed - jnp.mean(summed, axis=-1, keepdims=True)
    inverse = lax.rsqrt(jnp.mean(center * center, axis=-1, keepdims=True) + norm_epsilon)
    normed = center * inverse
    return (normed * gain.astype(jnp.float32) + shift.astype(jnp.float32), normed, inverse)


def norm_backward(grad_out, gain, normed, inverse):
    scaled = grad_out * gain.astype(jnp.float32)
    grad_in = inverse * (
        scaled
        - jnp.mean(scaled, axis=-1, keepdims=True)
        - normed * jnp.mean(scaled * normed, axis=-1, keepdims=True)
    )
    return (grad_in, jnp.sum(grad_out * normed, axis=0), jnp.sum(grad_out, axis=0))


def block_layout(seq_len):
    block_rows = min(512, seq_len)
    return (block_rows, seq_len // block_rows)


def attend_sequence(item):
    queries, keys_seq, values_seq, length = item
    seq_len = queries.shape[0]
    block_rows, block_count = block_layout(seq_len)
    score_scale = HEAD_DIM ** (-0.5)
    valid_keys = jnp.arange(seq_len, dtype=jnp.int32) < length
    heads_k = keys_seq.reshape(seq_len, HEADS, HEAD_DIM)
    heads_v = values_seq.reshape(seq_len, HEADS, HEAD_DIM)

    def one_block(query_block):
        scores = (
            jnp.einsum("qhd,khd->hqk", query_block, heads_k, preferred_element_type=jnp.float32)
            * score_scale
        )
        scores = jnp.where(valid_keys[None, None, :], scores, masked_score)
        highest = jnp.max(scores, axis=-1, keepdims=True)
        exponent = jnp.exp(scores - highest)
        totals = jnp.sum(exponent, axis=-1, keepdims=True)
        weights_low = (exponent / totals).astype(jnp.bfloat16)
        context = jnp.einsum(
            "hqk,khd->qhd", weights_low, heads_v, preferred_element_type=jnp.float32
        )
        return (
            context.astype(jnp.bfloat16).reshape(block_rows, HEADS * HEAD_DIM),
            (highest + jnp.log(totals))[..., 0],
        )

    blocks = queries.reshape(block_count, block_rows, HEADS, HEAD_DIM)
    context, logsum = lax.map(one_block, blocks)
    return (context.reshape(seq_len, HEADS * HEAD_DIM), logsum)


def attend_backward(item):
    queries, keys_seq, values_seq, length, logsum, grad_context = item
    seq_len = queries.shape[0]
    block_rows, block_count = block_layout(seq_len)
    score_scale = HEAD_DIM ** (-0.5)
    valid_keys = jnp.arange(seq_len, dtype=jnp.int32) < length
    heads_k = keys_seq.reshape(seq_len, HEADS, HEAD_DIM)
    heads_v = values_seq.reshape(seq_len, HEADS, HEAD_DIM)
    query_blocks = queries.reshape(block_count, block_rows, HEADS, HEAD_DIM)
    grad_blocks = grad_context.reshape(block_count, block_rows, HEADS, HEAD_DIM)

    def block_step(carry, piece):
        grad_keys, grad_values = carry
        query_block, grad_block, logsum_block = piece
        scores = (
            jnp.einsum("qhd,khd->hqk", query_block, heads_k, preferred_element_type=jnp.float32)
            * score_scale
        )
        scores = jnp.where(valid_keys[None, None, :], scores, masked_score)
        weights = jnp.exp(scores - logsum_block[..., None])
        weights_low = weights.astype(jnp.bfloat16)
        grad_values = grad_values + jnp.einsum(
            "hqk,qhd->khd", weights_low, grad_block, preferred_element_type=jnp.float32
        )
        grad_weights = jnp.einsum(
            "qhd,khd->hqk", grad_block, heads_v, preferred_element_type=jnp.float32
        )
        grad_scores = weights * (
            grad_weights - jnp.sum(weights * grad_weights, axis=-1, keepdims=True)
        )
        grad_scores = grad_scores.astype(jnp.bfloat16)
        grad_query = (
            jnp.einsum("hqk,khd->qhd", grad_scores, heads_k, preferred_element_type=jnp.float32)
            * score_scale
        )
        grad_keys = (
            grad_keys
            + jnp.einsum(
                "hqk,qhd->khd", grad_scores, query_block, preferred_element_type=jnp.float32
            )
            * score_scale
        )
        return ((grad_keys, grad_values), grad_query)

    zeros = jnp.zeros((seq_len, HEADS, HEAD_DIM), jnp.float32)
    (grad_keys, grad_values), grad_query = lax.scan(
        block_step, (zeros, zeros), (query_blocks, grad_blocks, logsum)
    )
    width = HEADS * HEAD_DIM
    return (
        grad_query.reshape(seq_len, width).astype(jnp.bfloat16),
        grad_keys.reshape(seq_len, width).astype(jnp.bfloat16),
        grad_values.reshape(seq_len, width).astype(jnp.bfloat16),
    )


def regroup(full):
    shard_count = lax.axis_size("shard")
    replica_count = lax.axis_size("replica")
    shape = full.shape
    split = full.reshape(
        (shard_count, replica_count, shape[0] // (shard_count * replica_count)) + shape[1:]
    )
    return jnp.swapaxes(split, 0, 1).reshape(shape)


def reduce_ffn(g_we, g_be, g_wc, g_bc, g_gb, g_sb, g_wp):
    p_we, p_be, p_wc, p_bc, p_gb, p_sb, p_wp = (
        lax.psum_scatter(regroup(g_we), ("replica", "shard"), scatter_dimension=0, tiled=True),
        lax.psum_scatter(regroup(g_be), ("replica", "shard"), scatter_dimension=0, tiled=True),
        lax.psum_scatter(regroup(g_wc), ("replica", "shard"), scatter_dimension=0, tiled=True),
        lax.psum_scatter(regroup(g_bc), ("replica", "shard"), scatter_dimension=0, tiled=True),
        lax.psum_scatter(regroup(g_gb), ("replica", "shard"), scatter_dimension=0, tiled=True),
        lax.psum_scatter(regroup(g_sb), ("replica", "shard"), scatter_dimension=0, tiled=True),
        lax.psum_scatter(regroup(g_wp), ("replica", "shard"), scatter_dimension=0, tiled=True),
    )
    return (
        lax.all_gather(p_we.astype(jnp.bfloat16), "replica", axis=0, tiled=True).astype(p_we.dtype),
        lax.all_gather(p_be.astype(jnp.bfloat16), "replica", axis=0, tiled=True).astype(p_be.dtype),
        lax.all_gather(p_wc.astype(jnp.bfloat16), "replica", axis=0, tiled=True).astype(p_wc.dtype),
        lax.all_gather(p_bc.astype(jnp.bfloat16), "replica", axis=0, tiled=True).astype(p_bc.dtype),
        lax.all_gather(p_gb.astype(jnp.bfloat16), "replica", axis=0, tiled=True).astype(p_gb.dtype),
        lax.all_gather(p_sb.astype(jnp.bfloat16), "replica", axis=0, tiled=True).astype(p_sb.dtype),
        lax.all_gather(p_wp.astype(jnp.bfloat16), "replica", axis=0, tiled=True).astype(p_wp.dtype),
    )


def reduce_attn(g_wq, g_bq, g_wk, g_wv, g_bv, g_wo, g_bo, g_ga, g_sa):
    p_wq, p_bq, p_wk, p_wv, p_bv, p_wo, p_bo, p_ga, p_sa = (
        lax.psum_scatter(regroup(g_wq), ("replica", "shard"), scatter_dimension=0, tiled=True),
        lax.psum_scatter(regroup(g_bq), ("replica", "shard"), scatter_dimension=0, tiled=True),
        lax.psum_scatter(regroup(g_wk), ("replica", "shard"), scatter_dimension=0, tiled=True),
        lax.psum_scatter(regroup(g_wv), ("replica", "shard"), scatter_dimension=0, tiled=True),
        lax.psum_scatter(regroup(g_bv), ("replica", "shard"), scatter_dimension=0, tiled=True),
        lax.psum_scatter(regroup(g_wo), ("replica", "shard"), scatter_dimension=0, tiled=True),
        lax.psum_scatter(regroup(g_bo), ("replica", "shard"), scatter_dimension=0, tiled=True),
        lax.psum_scatter(regroup(g_ga), ("replica", "shard"), scatter_dimension=0, tiled=True),
        lax.psum_scatter(regroup(g_sa), ("replica", "shard"), scatter_dimension=0, tiled=True),
    )
    return (
        lax.all_gather(p_wq.astype(jnp.bfloat16), "replica", axis=0, tiled=True).astype(p_wq.dtype),
        lax.all_gather(p_bq.astype(jnp.bfloat16), "replica", axis=0, tiled=True).astype(p_bq.dtype),
        lax.all_gather(p_wk.astype(jnp.bfloat16), "replica", axis=0, tiled=True).astype(p_wk.dtype),
        lax.all_gather(p_wv.astype(jnp.bfloat16), "replica", axis=0, tiled=True).astype(p_wv.dtype),
        lax.all_gather(p_bv.astype(jnp.bfloat16), "replica", axis=0, tiled=True).astype(p_bv.dtype),
        lax.all_gather(p_wo.astype(jnp.bfloat16), "replica", axis=0, tiled=True).astype(p_wo.dtype),
        lax.all_gather(p_bo.astype(jnp.bfloat16), "replica", axis=0, tiled=True).astype(p_bo.dtype),
        lax.all_gather(p_ga.astype(jnp.bfloat16), "replica", axis=0, tiled=True).astype(p_ga.dtype),
        lax.all_gather(p_sa.astype(jnp.bfloat16), "replica", axis=0, tiled=True).astype(p_sa.dtype),
    )


def per_device(
    tokens,
    lengths,
    w_query,
    b_query,
    w_key,
    w_value,
    b_value,
    w_attn_out,
    b_attn_out,
    gain_one,
    shift_one,
    w_expand,
    b_expand,
    w_contract,
    b_contract,
    gain_two,
    shift_two,
    w_colbert,
    cotangent,
):
    seq_count, seq_len, width = tokens.shape
    row_count = seq_count * seq_len
    attn_full = (
        lax.all_gather(w_query, "shard", axis=0, tiled=True),
        lax.all_gather(b_query, "shard", axis=0, tiled=True),
        lax.all_gather(w_key, "shard", axis=0, tiled=True),
        lax.all_gather(w_value, "shard", axis=0, tiled=True),
        lax.all_gather(b_value, "shard", axis=0, tiled=True),
        lax.all_gather(w_attn_out, "shard", axis=0, tiled=True),
        lax.all_gather(b_attn_out, "shard", axis=0, tiled=True),
        lax.all_gather(gain_one, "shard", axis=0, tiled=True),
        lax.all_gather(shift_one, "shard", axis=0, tiled=True),
    )
    ffn_full = (
        lax.all_gather(w_expand, "shard", axis=0, tiled=True),
        lax.all_gather(b_expand, "shard", axis=0, tiled=True),
        lax.all_gather(w_contract, "shard", axis=0, tiled=True),
        lax.all_gather(b_contract, "shard", axis=0, tiled=True),
        lax.all_gather(gain_two, "shard", axis=0, tiled=True),
        lax.all_gather(shift_two, "shard", axis=0, tiled=True),
        lax.all_gather(w_colbert, "shard", axis=0, tiled=True),
    )
    query_w, query_b, key_w, value_w, value_b, out_w, out_b, gain_a, shift_a = attn_full
    expand_w, expand_b, contract_w, contract_b, gain_b, shift_b, colbert_w = ffn_full
    inputs = tokens.reshape(row_count, width)
    positions = jnp.arange(seq_len, dtype=jnp.int32)
    valid_f = (positions[None, :] < lengths[:, None]).astype(jnp.float32).reshape(row_count, 1)
    queries = (product(inputs, query_w) + query_b.astype(jnp.float32)).astype(jnp.bfloat16)
    keys_all = product(inputs, key_w).astype(jnp.bfloat16)
    values_all = (product(inputs, value_w) + value_b.astype(jnp.float32)).astype(jnp.bfloat16)
    seq_shape = (seq_count, seq_len, width)
    context, logsum = lax.map(
        attend_sequence,
        (
            queries.reshape(seq_shape),
            keys_all.reshape(seq_shape),
            values_all.reshape(seq_shape),
            lengths,
        ),
    )
    context = context.reshape(row_count, width)
    attended = product(context, out_w) + out_b.astype(jnp.float32)
    inputs_f = inputs.astype(jnp.float32)
    hidden_one, normed_one, inverse_one = layer_norm(inputs_f + attended, gain_a, shift_a)
    hidden_low = hidden_one.astype(jnp.bfloat16)
    expanded = product(hidden_low, expand_w) + expand_b.astype(jnp.float32)
    activated = jax.nn.gelu(expanded, approximate=False).astype(jnp.bfloat16)
    contracted = product(activated, contract_w) + contract_b.astype(jnp.float32)
    hidden_two, normed_two, inverse_two = layer_norm(hidden_one + contracted, gain_b, shift_b)
    hidden_two_low = hidden_two.astype(jnp.bfloat16)
    projected = product(hidden_two_low, colbert_w)
    inverse_len = lax.rsqrt(jnp.sum(projected * projected, axis=-1, keepdims=True) + norm_epsilon)
    normalized = projected * inverse_len
    embeddings = (normalized * valid_f).astype(jnp.bfloat16).reshape(seq_count, seq_len, -1)
    squares = jnp.stack(
        [
            jnp.sum(inputs_f * inputs_f * valid_f),
            jnp.sum(attended * attended * valid_f),
            jnp.sum(contracted * contracted * valid_f),
        ]
    )
    sums, count = lax.psum((squares, jnp.sum(valid_f)), ("replica", "shard"))
    rms_values = jnp.sqrt(sums / (count * width))
    ffn_back = (
        lax.all_gather(w_expand, "shard", axis=0, tiled=True),
        lax.all_gather(b_expand, "shard", axis=0, tiled=True),
        lax.all_gather(w_contract, "shard", axis=0, tiled=True),
        lax.all_gather(b_contract, "shard", axis=0, tiled=True),
        lax.all_gather(gain_two, "shard", axis=0, tiled=True),
        lax.all_gather(shift_two, "shard", axis=0, tiled=True),
        lax.all_gather(w_colbert, "shard", axis=0, tiled=True),
    )
    attn_back = (
        lax.all_gather(w_query, "shard", axis=0, tiled=True),
        lax.all_gather(b_query, "shard", axis=0, tiled=True),
        lax.all_gather(w_key, "shard", axis=0, tiled=True),
        lax.all_gather(w_value, "shard", axis=0, tiled=True),
        lax.all_gather(b_value, "shard", axis=0, tiled=True),
        lax.all_gather(w_attn_out, "shard", axis=0, tiled=True),
        lax.all_gather(b_attn_out, "shard", axis=0, tiled=True),
        lax.all_gather(gain_one, "shard", axis=0, tiled=True),
        lax.all_gather(shift_one, "shard", axis=0, tiled=True),
    )
    query_w, query_b, key_w, value_w, value_b, out_w, out_b, gain_a, shift_a = attn_back
    expand_w, expand_b, contract_w, contract_b, gain_b, shift_b, colbert_w = ffn_back
    grad_norm = cotangent.reshape(row_count, -1).astype(jnp.float32) * valid_f
    grad_projected = (
        inverse_len
        * (grad_norm - normalized * jnp.sum(normalized * grad_norm, axis=-1, keepdims=True))
    ).astype(jnp.bfloat16)
    grad_colbert = product_left_t(hidden_two_low, grad_projected)
    grad_hidden_two = product_right_t(grad_projected, colbert_w)
    grad_sum_two, grad_gain_two, grad_shift_two = norm_backward(
        grad_hidden_two, gain_b, normed_two, inverse_two
    )
    grad_contracted = grad_sum_two.astype(jnp.bfloat16)
    grad_contract_b = jnp.sum(grad_contracted, axis=0, dtype=jnp.float32)
    grad_contract_w = product_left_t(activated, grad_contracted)
    grad_activated = product_right_t(grad_contracted, contract_w)
    unused, gelu_back = jax.vjp(partial(jax.nn.gelu, approximate=False), expanded)
    grad_expanded = gelu_back(grad_activated)[0].astype(jnp.bfloat16)
    grad_expand_b = jnp.sum(grad_expanded, axis=0, dtype=jnp.float32)
    grad_expand_w = product_left_t(hidden_low, grad_expanded)
    ffn_grads = reduce_ffn(
        grad_expand_w,
        grad_expand_b,
        grad_contract_w,
        grad_contract_b,
        grad_gain_two,
        grad_shift_two,
        grad_colbert,
    )
    grad_hidden_one = grad_sum_two + product_right_t(grad_expanded, expand_w)
    grad_sum_one, grad_gain_one, grad_shift_one = norm_backward(
        grad_hidden_one, gain_a, normed_one, inverse_one
    )
    grad_attended = grad_sum_one.astype(jnp.bfloat16)
    grad_out_b = jnp.sum(grad_attended, axis=0, dtype=jnp.float32)
    grad_out_w = product_left_t(context, grad_attended)
    grad_context = product_right_t(grad_attended, out_w).astype(jnp.bfloat16)
    grad_queries, grad_keys, grad_values = lax.map(
        attend_backward,
        (
            queries.reshape(seq_shape),
            keys_all.reshape(seq_shape),
            values_all.reshape(seq_shape),
            lengths,
            logsum,
            grad_context.reshape(seq_shape),
        ),
    )
    grad_queries = grad_queries.reshape(row_count, width)
    grad_keys = grad_keys.reshape(row_count, width)
    grad_values = grad_values.reshape(row_count, width)
    grad_query_b = jnp.sum(grad_queries, axis=0, dtype=jnp.float32)
    grad_value_b = jnp.sum(grad_values, axis=0, dtype=jnp.float32)
    grad_query_w = product_left_t(inputs, grad_queries)
    grad_key_w = product_left_t(inputs, grad_keys)
    grad_value_w = product_left_t(inputs, grad_values)
    attn_grads = reduce_attn(
        grad_query_w,
        grad_query_b,
        grad_key_w,
        grad_value_w,
        grad_value_b,
        grad_out_w,
        grad_out_b,
        grad_gain_one,
        grad_shift_one,
    )
    grad_inputs = (
        grad_sum_one
        + product_right_t(grad_queries, query_w)
        + product_right_t(grad_keys, key_w)
        + product_right_t(grad_values, value_w)
    )
    grad_tokens = grad_inputs.astype(jnp.bfloat16).reshape(seq_count, seq_len, width)
    r_wq, r_bq, r_wk, r_wv, r_bv, r_wo, r_bo, r_ga, r_sa = attn_grads
    r_we, r_be, r_wc, r_bc, r_gb, r_sb, r_wp = ffn_grads
    return (
        embeddings,
        grad_tokens,
        r_wq,
        r_bq,
        r_wk,
        r_wv,
        r_bv,
        r_wo,
        r_bo,
        r_ga,
        r_sa,
        r_we,
        r_be,
        r_wc,
        r_bc,
        r_gb,
        r_sb,
        r_wp,
        rms_values,
    )


def solution(mesh):
    placed = (
        P(("replica", "shard"), None, None),
        P(("replica", "shard")),
        P("shard", None),
        P("shard"),
        P("shard", None),
        P("shard", None),
        P("shard"),
        P("shard", None),
        P("shard"),
        P("shard"),
        P("shard"),
        P("shard", None),
        P("shard"),
        P("shard", None),
        P("shard"),
        P("shard"),
        P("shard"),
        P("shard", None),
        P(("replica", "shard"), None, None),
    )
    return jax.shard_map(
        per_device,
        mesh=mesh,
        in_specs=placed,
        out_specs=(
            P(("replica", "shard"), None, None),
            P(("replica", "shard"), None, None),
            P("shard", None),
            P("shard"),
            P("shard", None),
            P("shard", None),
            P("shard"),
            P("shard", None),
            P("shard"),
            P("shard"),
            P("shard"),
            P("shard", None),
            P("shard"),
            P("shard", None),
            P("shard"),
            P("shard"),
            P("shard"),
            P("shard", None),
            P(),
        ),
        check_vma=False,
    )
```

profile of v0, /device:TPU:0, one launch (start us, length us, event | category | flops | bytes accessed | tf_op | source)
XLA Modules:
  0.0 1148.0 jit_solution(13677705353163011645)
XLA Ops:
  14.5 17.6 %all-reduce.29 = (bf16[768]{0:T(1024)(128)(2,1)S(1)}, bf16[768]{0:T(1024)(128)(2,1)S(1)}, bf16[768]{0:T(1024)(128)(2,1)S(1)}, bf16[768]{0:T(1024)(128)(2,1)S(1)}...) all-reduce(bf16[768]{0:T(1024)(128)(2,1)S(1)} %dynamic-update-slice, ...), channel_id=1, replica_groups=mesh['replica'=8,'shard'=4] {'shard'}, use_global_device_ids=true, to_apply=%add | all-reduce | flops 6144 | bytes 24576
  56.0 14.2 %all-gather.10.cloned.1.call-done = bf16[768,768]{1,0:T(8,128)(2,1)} async-done(((bf16[192,768]{1,0:T(8,128)(2,1)}), bf16[768,768]{1,0:T(8,128)(2,1)}) %all-gather.10.cloned.1.call-update) | async-done | bytes 1179664 | tf_op jit(solution)/shard_map/all_gather | solution.py:225
  75.7 24.1 %all-gather.14.cloned.1.call-done = bf16[768,768]{1,0:T(8,128)(2,1)} async-done(((bf16[192,768]{1,0:T(8,128)(2,1)}), bf16[768,768]{1,0:T(8,128)(2,1)}) %all-gather.14.cloned.1.call-update) | async-done | bytes 1179664 | tf_op jit(solution)/shard_map/all_gather | solution.py:224
  106.2 26.2 %while.10 = (s32[]{:T(128)}, bf16[2,512,768]{2,1,0:T(8,128)(2,1)}, f32[2,1,12,512]{3,2,1,0:T(8,128)S(1)}, bf16[2,512,768]{1,2,0:T(8,128)(2,1)S(1)}, s32[2]{0:T(1...) while((s32[]{:T(128)}, bf16[2,512,768]{2,1,0:T(8,128)(2,1)}, ...), condition=%wide.region_3.4_spmd, body=%wide.region_0.3_spmd.sunk | while | flops 843442688 | bytes 48982140 | solution.py:250
  140.5 47.5 %all-gather.18.cloned.1.call-done = bf16[768,3072]{1,0:T(8,128)(2,1)} async-done(((bf16[192,3072]{1,0:T(8,128)(2,1)}), bf16[768,3072]{1,0:T(8,128)(2,1)}) %all-gather.18.cloned.1.call-update) | async-done | bytes 4718608 | tf_op jit(solution)/shard_map/all_gather | solution.py:233
  188.0 38.3 %multiply_convert_fusion.3 = (bf16[1024,3072]{1,0:T(8,128)(2,1)}, f32[1024,3072]{1,0:T(8,128)}, f32[1024,3072]{1,0:T(8,128)}) fusion(f32[3072]{0:T(1024)S(1)} %bitcast.264, bf16[768,3072]{1,0:T(8,128)(2,1)} %all-gather.18.cloned.1.call-done, f32[1024,768]{1,0:T(8,128)} %copy-done.1, f32[768]{0:T(1024)S(1)} %convert_element_type.282, ...), kind=kOutput, calls=%fused_computation.39 | convolution fusion | flops 5043388416 | bytes 39348224 | tf_op jit(solution)/shard_map/dot_general | solution.py:17
  226.4 20.5 %all-gather.20.cloned.1.call-done = bf16[3072,768]{1,0:T(8,128)(2,1)} async-done(((bf16[768,768]{1,0:T(8,128)(2,1)}), bf16[3072,768]{1,0:T(8,128)(2,1)}) %all-gather.20.cloned.1.call-update) | async-done | bytes 4718608 | tf_op jit(solution)/shard_map/all_gather | solution.py:235
  266.5 19.4 %convert_reduce_fusion = (f32[3072]{0:T(1024)}, bf16[1024,3072]{1,0:T(8,128)(2,1)}) fusion(f32[1024,3072]{1,0:T(8,128)} %get-tuple-element.314, bf16[3072,768]{1,0:T(8,128)(2,1)} %all-gather.20.cloned.1.call-done, f32[1024,768]{1,0:T(8,128)} %get-tuple-element.308, f32[1024,3072]{1,0:T(8,128)} %get-tuple-element.332, f32[3072]{0:T(1024)S(1)} %bitcast.265), kind=kOutput, calls=%fused_computation.37 | convolution fusion | flops 4886098944 | bytes 39346176 | tf_op jit(solution)/shard_map/dot_general | solution.py:27
  340.3 65.1 %while.27 = (s32[]{:T(128)}, bf16[2,512,768]{1,2,0:T(8,128)(2,1)}, bf16[2,512,768]{1,2,0:T(8,128)(2,1)}, bf16[2,512,768]{1,2,0:T(8,128)(2,1)}, bf16[2,512,768]{1...) while((s32[]{:T(128)}, bf16[2,512,768]{1,2,0:T(8,128)(2,1)}, ...), condition=%wide.region_16.17_spmd, body=%wide.region_14.16_spmd.sunk | while | flops 2062412288 | bytes 152742224 | solution.py:339
  419.7 13.9 %reduce-scatter.18.cloned.1.call-done = f32[24,3072]{1,0:T(8,128)} async-done(((f32[768,3072]{1,0:T(8,128)}), f32[24,3072]{1,0:T(8,128)}) %reduce-scatter.18.cloned.1.call-update) | async-done | bytes 294928 | tf_op jit(solution)/shard_map/reduce_scatter | solution.py:154
  445.3 41.4 %all-reduce.27 = (bf16[768]{0:T(1024)(128)(2,1)S(1)}, bf16[768]{0:T(1024)(128)(2,1)S(1)}, bf16[768]{0:T(1024)(128)(2,1)S(1)}, bf16[768]{0:T(1024)(128)(2,1)S(1)}...) all-reduce(f32[768]{0:T(1024)S(1)} %reshape.368, ...), channel_id=3, replica_groups=mesh['replica'=8,'shard'=4] {'replica','shard'}, use_global_device_ids=true, to_apply=%region_19.20.clone | all-reduce | flops 9220 | bytes 55328
  487.4 88.0 %reduce-scatter.20.cloned.1.call-done = f32[96,768]{1,0:T(8,128)} async-done(((f32[3072,768]{1,0:T(8,128)}), f32[96,768]{1,0:T(8,128)}) %reduce-scatter.20.cloned.1.call-update) | async-done | bytes 294928 | tf_op jit(solution)/shard_map/reduce_scatter | solution.py:156
  585.9 14.0 %all-reduce.28 = (bf16[192]{0:T(256)(128)(2,1)S(1)}, bf16[192]{0:T(256)(128)(2,1)S(1)}, bf16[192]{0:T(256)(128)(2,1)S(1)}, bf16[192]{0:T(256)(128)(2,1)S(1)}, bf...) all-reduce(bf16[192]{0:T(256)(128)(2,1)S(1)} %dynamic-update-slice., ...), channel_id=1, replica_groups=mesh['replica'=8,'shard'=4] {'replica'}, use_global_device_ids=true, to_apply=%add.8 | all-reduce | flops 2304 | bytes 9216
  613.2 61.5 %reduce-scatter.22.cloned.1.call-done = f32[24,128]{1,0:T(8,128)} async-done(((f32[768,128]{1,0:T(8,128)}), f32[24,128]{1,0:T(8,128)}) %reduce-scatter.22.cloned.1.call-update) | async-done | bytes 12304
  675.5 14.0 %all_gather.136 = bf16[192,128]{1,0:T(8,128)(2,1)S(1)} all-gather(bf16[24,128]{1,0:T(8,128)(2,1)S(1)} %convert_element_type.336), channel_id=1, replica_groups=mesh['replica'=8,'shard'=4] {'replica'}, dimensions={0}, use_global_device_ids=true | all-gather | bytes 55296 | tf_op jit(solution)/shard_map/all_gather | solution.py:169
  690.1 88.7 %reduce-scatter.16.cloned.1.call-done = f32[24,768]{1,0:T(8,128)} async-done(((f32[768,768]{1,0:T(8,128)}), f32[24,768]{1,0:T(8,128)}) %reduce-scatter.16.cloned.1.call-update) | async-done | bytes 73744 | tf_op jit(solution)/shard_map/reduce_scatter | solution.py:180
  779.6 14.3 %all_gather.126 = bf16[192,768]{1,0:T(8,128)(2,1)S(1)} all-gather(bf16[24,768]{1,0:T(8,128)(2,1)S(1)} %convert_element_type.313), channel_id=1, replica_groups=mesh['replica'=8,'shard'=4] {'replica'}, dimensions={0}, use_global_device_ids=true | all-gather | bytes 331776 | tf_op jit(solution)/shard_map/all_gather | solution.py:191
  794.8 88.0 %reduce-scatter.12.cloned.1.call-done = f32[24,768]{1,0:T(8,128)} async-done(((f32[768,768]{1,0:T(8,128)}), f32[24,768]{1,0:T(8,128)}) %reduce-scatter.12.cloned.1.call-update) | async-done | bytes 73744 | tf_op jit(solution)/shard_map/reduce_scatter | solution.py:177
  883.6 14.3 %all_gather.123 = bf16[192,768]{1,0:T(8,128)(2,1)S(1)} all-gather(bf16[24,768]{1,0:T(8,128)(2,1)S(1)} %convert_element_type.306), channel_id=1, replica_groups=mesh['replica'=8,'shard'=4] {'replica'}, dimensions={0}, use_global_device_ids=true | all-gather | bytes 331776 | tf_op jit(solution)/shard_map/all_gather | solution.py:188
  898.7 88.0 %reduce-scatter.14.cloned.1.call-done = f32[24,768]{1,0:T(8,128)} async-done(((f32[768,768]{1,0:T(8,128)}), f32[24,768]{1,0:T(8,128)}) %reduce-scatter.14.cloned.1.call-update) | async-done | bytes 73744 | tf_op jit(solution)/shard_map/reduce_scatter | solution.py:178
  987.7 14.3 %all_gather.124 = bf16[192,768]{1,0:T(8,128)(2,1)S(1)} all-gather(bf16[24,768]{1,0:T(8,128)(2,1)S(1)} %convert_element_type.308), channel_id=1, replica_groups=mesh['replica'=8,'shard'=4] {'replica'}, dimensions={0}, use_global_device_ids=true | all-gather | bytes 331776 | tf_op jit(solution)/shard_map/all_gather | solution.py:189
  1002.8 88.0 %reduce-scatter.10.cloned.1.call-done = f32[24,768]{1,0:T(8,128)} async-done(((f32[768,768]{1,0:T(8,128)}), f32[24,768]{1,0:T(8,128)}) %reduce-scatter.10.cloned.1.call-update) | async-done | bytes 73744 | tf_op jit(solution)/shard_map/reduce_scatter | solution.py:175
  1091.6 14.7 %all_gather.121 = bf16[192,768]{1,0:T(8,128)(2,1)S(1)} all-gather(bf16[24,768]{1,0:T(8,128)(2,1)S(1)} %convert_element_type.301), channel_id=1, replica_groups=mesh['replica'=8,'shard'=4] {'replica'}, dimensions={0}, use_global_device_ids=true | all-gather | bytes 331776 | tf_op jit(solution)/shard_map/all_gather | solution.py:186
  1117.3 21.1 %all-gather.24.cloned.1.call-done = bf16[768,768]{1,0:T(8,128)(2,1)} async-done(((bf16[96,768]{1,0:T(8,128)(2,1)}), bf16[768,768]{1,0:T(8,128)(2,1)}) %all-gather.24.cloned.1.call-update) | async-done | bytes 1179664 | tf_op jit(solution)/shard_map/all_gather | solution.py:165
  (371 shorter events, 284.2 us)
Async XLA Ops:
  7.3 24.8 %copy-start.39 = (bf16[768]{0:T(1024)(128)(2,1)S(1)}, bf16[768]{0:T(1024)(128)(2,1)}, u32[]{:S(2)}) copy-start(bf16[768]{0:T(1024)(128)(2,1)} %param.35) | copy-start | bytes 4612
  7.3 26.6 %copy-start.40 = (s32[2]{0:T(128)S(1)}, s32[2]{0:T(128)}, u32[]{:S(2)}) copy-start(s32[2]{0:T(128)} %param.24) | copy-start | bytes 28
  7.3 35.1 %copy-start.26 = (bf16[192,128]{1,0:T(8,128)(2,1)S(1)}, bf16[192,128]{1,0:T(8,128)(2,1)}, u32[]{:S(2)}) copy-start(bf16[192,128]{1,0:T(8,128)(2,1)} %param.40) | copy-start | bytes 147460
  7.3 44.4 %copy-start.12 = (bf16[2,512,768]{2,1,0:T(8,128)(2,1)S(1)}, bf16[2,512,768]{2,1,0:T(8,128)(2,1)}, u32[]{:S(2)}) copy-start(bf16[2,512,768]{2,1,0:T(8,128)(2,1)} %param.23) | copy-start | bytes 4718596
  7.3 44.4 %all-gather.12.cloned.1.call-start = ((), (), s32[]{:S(2)}) async-start(), calls=%async_computation.8 | async-start | bytes 1474560 | tf_op jit(solution)/shard_map/all_gather | solution.py:222
  8.1 62.1 %all-gather.10.cloned.1.call-start = ((), (), s32[]{:S(2)}) async-start(), calls=%async_computation.7 | async-start | bytes 1474560 | tf_op jit(solution)/shard_map/all_gather | solution.py:225
  8.8 91.0 %all-gather.14.cloned.1.call-start = ((), (), s32[]{:S(2)}) async-start(), calls=%async_computation.9 | async-start | bytes 1474560 | tf_op jit(solution)/shard_map/all_gather | solution.py:224
  9.5 122.9 %all-gather.16.cloned.1.call-start = ((), (), s32[]{:S(2)}) async-start(), calls=%async_computation.10 | async-start | bytes 1474560 | tf_op jit(solution)/shard_map/all_gather | solution.py:227
  10.1 177.9 %all-gather.18.cloned.1.call-start = ((), (), s32[]{:S(2)}) async-start(), calls=%async_computation.11 | async-start | bytes 5898240 | tf_op jit(solution)/shard_map/all_gather | solution.py:233
  10.7 236.1 %all-gather.20.cloned.1.call-start = ((), (), s32[]{:S(2)}) async-start(), calls=%async_computation.12 | async-start | bytes 5898240 | tf_op jit(solution)/shard_map/all_gather | solution.py:235
  11.3 422.3 %reduce-scatter.18.cloned.1.call-start = ((), (), s32[]{:S(2)}) async-start(), calls=%async_computation.17 | async-start | bytes 9732096 | tf_op jit(solution)/shard_map/reduce_scatter | solution.py:154
  188.0 58.8 %copy-start.2 = (f32[1024,768]{1,0:T(8,128)S(1)}, f32[1024,768]{1,0:T(8,128)}, u32[]{:S(2)}) copy-start(f32[1024,768]{1,0:T(8,128)} %copy-done.1) | copy-start | bytes 9437188
  188.0 58.8 %copy-start.28 = (f32[1,4,2,128]{3,1,2,0:T(4,128)S(1)}, f32[1,4,2,128]{3,1,2,0:T(4,128)}, u32[]{:S(2)}) copy-start(f32[1,4,2,128]{3,1,2,0:T(4,128)} %copy.180) | copy-start | bytes 12292
  188.0 58.8 %copy-start.38 = (f32[768]{0:T(1024)S(1)}, f32[768]{0:T(1024)}, u32[]{:S(2)}) copy-start(f32[768]{0:T(1024)} %convert_element_type.286) | copy-start | bytes 9220
  298.1 277.3 %reduce-scatter.20.cloned.1.call-start = ((), (), s32[]{:S(2)}) async-start(), calls=%async_computation.19 | async-start | bytes 9732096 | tf_op jit(solution)/shard_map/reduce_scatter | solution.py:156
  311.4 363.4 %reduce-scatter.22.cloned.1.call-start = ((), (), s32[]{:S(2)}) async-start(), calls=%async_computation.21 | async-start | bytes 405504
  329.0 449.8 %reduce-scatter.16.cloned.1.call-start = ((), (), s32[]{:S(2)}) async-start(), calls=%async_computation.16 | async-start | bytes 2433024 | tf_op jit(solution)/shard_map/reduce_scatter | solution.py:180
  335.6 547.1 %reduce-scatter.12.cloned.1.call-start = ((), (), s32[]{:S(2)}) async-start(), calls=%async_computation.14 | async-start | bytes 2433024 | tf_op jit(solution)/shard_map/reduce_scatter | solution.py:177
  410.5 576.3 %reduce-scatter.14.cloned.1.call-start = ((), (), s32[]{:S(2)}) async-start(), calls=%async_computation.15 | async-start | bytes 2433024 | tf_op jit(solution)/shard_map/reduce_scatter | solution.py:178
  414.7 676.0 %reduce-scatter.10.cloned.1.call-start = ((), (), s32[]{:S(2)}) async-start(), calls=%async_computation.13 | async-start | bytes 2433024 | tf_op jit(solution)/shard_map/reduce_scatter | solution.py:175
  419.6 22.5 %copy-start.34 = (f32[768]{0:T(1024)S(1)}, f32[768]{0:T(1024)}, u32[]{:S(2)}) copy-start(f32[768]{0:T(1024)} %get-tuple-element.241) | copy-start | bytes 9220
  419.7 694.7 %all-gather.22.cloned.1.call-start = ((), (), s32[]{:S(2)}) async-start(), calls=%async_computation.18 | async-start | bytes 1327104 | tf_op jit(solution)/shard_map/all_gather | solution.py:163
  435.2 703.2 %all-gather.24.cloned.1.call-start = ((), (), s32[]{:S(2)}) async-start(), calls=%async_computation.20 | async-start | bytes 1327104 | tf_op jit(solution)/shard_map/all_gather | solution.py:165
  581.7 23.3 %copy-start.15 = (bf16[2,512,768]{2,1,0:T(8,128)(2,1)S(1)}, bf16[2,512,768]{2,1,0:T(8,128)(2,1)}, u32[]{:S(2)}) copy-start(bf16[2,512,768]{2,1,0:T(8,128)(2,1)} %copy.141) | copy-start | bytes 4718596
  (50 other events, 303.0 us)
Sparse Core Ops, SparseCore 0:
  10.0 30.5 all-gather.11
  42.4 27.7 all-gather.9
  72.0 27.7 all-gather.13
  101.5 27.7 all-gather.15
  131.0 57.0 all-gather.17
  189.7 57.0 all-gather.19
  298.2 135.3 reduce-scatter.17
  440.5 134.8 reduce-scatter.19
  580.9 93.8 reduce-scatter.21
  680.7 97.9 reduce-scatter.15
  784.6 98.0 reduce-scatter.11
  888.7 97.9 reduce-scatter.13
  992.6 98.0 reduce-scatter.9
  1092.3 22.0 all-gather.21
  1116.0 22.4 all-gather.23
where the time goes:
time: 1160 us; the launch traced here: 1150 us
  waiting for transfers between devices  654 us (56%)
  matrix products  182 us (16%)
  blocking collectives  161 us (14%)
  local copies, waits for them, and re-layouts  67.9 us (6%)
  other arithmetic  63.3 us (5%)
  between operations  17.6 us (2%)
    reduce_scatter x1, waiting for transfers between devices, reduce_attn(): lax.psum_scatter(regroup(g_wo), ('replica', 'shard'), scatter_dimension=0...  88.7 us
    reduce_scatter x1, waiting for transfers between devices, reduce_attn(): lax.psum_scatter(regroup(g_wv), ('replica', 'shard'), scatter_dimension=0...  88 us
    reduce_scatter x1, waiting for transfers between devices, reduce_ffn(): lax.psum_scatter(regroup(g_wc), ('replica', 'shard'), scatter_dimension=0...  88 us
    reduce_scatter x1, waiting for transfers between devices, reduce_attn(): lax.psum_scatter(regroup(g_wk), ('replica', 'shard'), scatter_dimension=0...  88 us
    reduce_scatter x1, waiting for transfers between devices, reduce_attn(): lax.psum_scatter(regroup(g_wq), ('replica', 'shard'), scatter_dimension=0...  88 us
    unnamed x3, blocking collectives  73 us
    dot_general x7, matrix products, product(): return jnp.dot(left, right, preferred_element_type=jnp.float32)  66.3 us
    unnamed x16, waiting for transfers between devices  65.3 us
  transfers between devices with their start and end apart: 15, of which 13 were waited for; matrix products, arithmetic and copies ran while one was open for 22% of the time, Pallas kernels for 0%

commit v1 on v0

--- a/solution.py
+++ b/solution.py
@@ -139,60 +139,74 @@
     )
 
 
-def regroup(full):
-    shard_count = lax.axis_size("shard")
-    replica_count = lax.axis_size("replica")
-    shape = full.shape
-    split = full.reshape(
-        (shard_count, replica_count, shape[0] // (shard_count * replica_count)) + shape[1:]
-    )
-    return jnp.swapaxes(split, 0, 1).reshape(shape)
-
-
-def reduce_ffn(g_we, g_be, g_wc, g_bc, g_gb, g_sb, g_wp):
-    p_we, p_be, p_wc, p_bc, p_gb, p_sb, p_wp = (
-        lax.psum_scatter(regroup(g_we), ("replica", "shard"), scatter_dimension=0, tiled=True),
-        lax.psum_scatter(regroup(g_be), ("replica", "shard"), scatter_dimension=0, tiled=True),
-        lax.psum_scatter(regroup(g_wc), ("replica", "shard"), scatter_dimension=0, tiled=True),
-        lax.psum_scatter(regroup(g_bc), ("replica", "shard"), scatter_dimension=0, tiled=True),
-        lax.psum_scatter(regroup(g_gb), ("replica", "shard"), scatter_dimension=0, tiled=True),
-        lax.psum_scatter(regroup(g_sb), ("replica", "shard"), scatter_dimension=0, tiled=True),
-        lax.psum_scatter(regroup(g_wp), ("replica", "shard"), scatter_dimension=0, tiled=True),
-    )
-    return (
-        lax.all_gather(p_we.astype(jnp.bfloat16), "replica", axis=0, tiled=True).astype(p_we.dtype),
-        lax.all_gather(p_be.astype(jnp.bfloat16), "replica", axis=0, tiled=True).astype(p_be.dtype),
-        lax.all_gather(p_wc.astype(jnp.bfloat16), "replica", axis=0, tiled=True).astype(p_wc.dtype),
-        lax.all_gather(p_bc.astype(jnp.bfloat16), "replica", axis=0, tiled=True).astype(p_bc.dtype),
-        lax.all_gather(p_gb.astype(jnp.bfloat16), "replica", axis=0, tiled=True).astype(p_gb.dtype),
-        lax.all_gather(p_sb.astype(jnp.bfloat16), "replica", axis=0, tiled=True).astype(p_sb.dtype),
-        lax.all_gather(p_wp.astype(jnp.bfloat16), "replica", axis=0, tiled=True).astype(p_wp.dtype),
-    )
-
-
-def reduce_attn(g_wq, g_bq, g_wk, g_wv, g_bv, g_wo, g_bo, g_ga, g_sa):
-    p_wq, p_bq, p_wk, p_wv, p_bv, p_wo, p_bo, p_ga, p_sa = (
-        lax.psum_scatter(regroup(g_wq), ("replica", "shard"), scatter_dimension=0, tiled=True),
-        lax.psum_scatter(regroup(g_bq), ("replica", "shard"), scatter_dimension=0, tiled=True),
-        lax.psum_scatter(regroup(g_wk), ("replica", "shard"), scatter_dimension=0, tiled=True),
-        lax.psum_scatter(regroup(g_wv), ("replica", "shard"), scatter_dimension=0, tiled=True),
-        lax.psum_scatter(regroup(g_bv), ("replica", "shard"), scatter_dimension=0, tiled=True),
-        lax.psum_scatter(regroup(g_wo), ("replica", "shard"), scatter_dimension=0, tiled=True),
-        lax.psum_scatter(regroup(g_bo), ("replica", "shard"), scatter_dimension=0, tiled=True),
-        lax.psum_scatter(regroup(g_ga), ("replica", "shard"), scatter_dimension=0, tiled=True),
-        lax.psum_scatter(regroup(g_sa), ("replica", "shard"), scatter_dimension=0, tiled=True),
-    )
-    return (
-        lax.all_gather(p_wq.astype(jnp.bfloat16), "replica", axis=0, tiled=True).astype(p_wq.dtype),
-        lax.all_gather(p_bq.astype(jnp.bfloat16), "replica", axis=0, tiled=True).astype(p_bq.dtype),
-        lax.all_gather(p_wk.astype(jnp.bfloat16), "replica", axis=0, tiled=True).astype(p_wk.dtype),
-        lax.all_gather(p_wv.astype(jnp.bfloat16), "replica", axis=0, tiled=True).astype(p_wv.dtype),
-        lax.all_gather(p_bv.astype(jnp.bfloat16), "replica", axis=0, tiled=True).astype(p_bv.dtype),
-        lax.all_gather(p_wo.astype(jnp.bfloat16), "replica", axis=0, tiled=True).astype(p_wo.dtype),
-        lax.all_gather(p_bo.astype(jnp.bfloat16), "replica", axis=0, tiled=True).astype(p_bo.dtype),
-        lax.all_gather(p_ga.astype(jnp.bfloat16), "replica", axis=0, tiled=True).astype(p_ga.dtype),
-        lax.all_gather(p_sa.astype(jnp.bfloat16), "replica", axis=0, tiled=True).astype(p_sa.dtype),
-    )
+def shard_partners(distance):
+    return [(i, i ^ distance) for i in range(lax.axis_size("shard"))]
+
+
+def replica_partners(distance):
+    return [(i, i ^ distance) for i in range(lax.axis_size("replica"))]
+
+
+def gather_rows(own):
+    shards = lax.axis_size("shard")
+    mine = lax.axis_index("shard")
+    core = lax.axis_index("replica") % 2
+    rows, width = own.shape
+    half = rows // 2
+    sent = lax.dynamic_slice_in_dim(own, core * half, half, 0)
+    full = jnp.zeros((shards * rows, width), own.dtype)
+    full = lax.dynamic_update_slice_in_dim(full, own, mine * rows, 0)
+    for distance in range(1, shards):
+        near = lax.ppermute(sent, "shard", shard_partners(distance))
+        far = lax.ppermute(near, "replica", replica_partners(1))
+        start = (mine ^ distance) * rows
+        full = lax.dynamic_update_slice_in_dim(full, near, start + core * half, 0)
+        full = lax.dynamic_update_slice_in_dim(full, far, start + (1 - core) * half, 0)
+    return full
+
+
+def reduce_rows(part):
+    shards = lax.axis_size("shard")
+    replicas = lax.axis_size("replica")
+    mine = lax.axis_index("shard")
+    core = lax.axis_index("replica") % 2
+    half = part.shape[0] // (2 * shards)
+
+    def block(distance, which):
+        return lax.dynamic_slice_in_dim(part, ((mine ^ distance) * 2 + which) * half, half, 0)
+
+    given = jnp.concatenate([block(d, 1 - core) for d in range(shards)]).astype(jnp.bfloat16)
+    taken = lax.ppermute(given, "replica", replica_partners(1))
+    sums = [
+        block(d, core).astype(jnp.bfloat16).astype(jnp.float32)
+        + taken[d * half : (d + 1) * half].astype(jnp.float32)
+        for d in range(shards)
+    ]
+    total = sums[0]
+    for distance in range(1, shards):
+        total = total + lax.ppermute(
+            sums[distance].astype(jnp.bfloat16), "shard", shard_partners(distance)
+        ).astype(jnp.float32)
+    distance = 2
+    low = total.astype(jnp.bfloat16)
+    while distance < replicas:
+        other = lax.ppermute(low, "replica", replica_partners(distance))
+        low = (low.astype(jnp.float32) + other.astype(jnp.float32)).astype(jnp.bfloat16)
+        distance *= 2
+    other = lax.ppermute(low, "replica", replica_partners(1))
+    first = jnp.where(core == 0, low, other)
+    second = jnp.where(core == 0, other, low)
+    return jnp.concatenate([first, second]).astype(jnp.float32)
+
+
+def sum_everywhere(part):
+    for axis in ("replica", "shard"):
+        distance = 1
+        while distance < lax.axis_size(axis):
+            pairs = [(i, i ^ distance) for i in range(lax.axis_size(axis))]
+            part = part + lax.ppermute(part, axis, pairs)
+            distance *= 2
+    return part
 
 
 def per_device(
@@ -218,28 +232,27 @@
 ):
     seq_count, seq_len, width = tokens.shape
     row_count = seq_count * seq_len
-    attn_full = (
-        lax.all_gather(w_query, "shard", axis=0, tiled=True),
-        lax.all_gather(b_query, "shard", axis=0, tiled=True),
-        lax.all_gather(w_key, "shard", axis=0, tiled=True),
-        lax.all_gather(w_value, "shard", axis=0, tiled=True),
-        lax.all_gather(b_value, "shard", axis=0, tiled=True),
-        lax.all_gather(w_attn_out, "shard", axis=0, tiled=True),
-        lax.all_gather(b_attn_out, "shard", axis=0, tiled=True),
-        lax.all_gather(gain_one, "shard", axis=0, tiled=True),
-        lax.all_gather(shift_one, "shard", axis=0, tiled=True),
-    )
-    ffn_full = (
-        lax.all_gather(w_expand, "shard", axis=0, tiled=True),
-        lax.all_gather(b_expand, "shard", axis=0, tiled=True),
-        lax.all_gather(w_contract, "shard", axis=0, tiled=True),
-        lax.all_gather(b_contract, "shard", axis=0, tiled=True),
-        lax.all_gather(gain_two, "shard", axis=0, tiled=True),
-        lax.all_gather(shift_two, "shard", axis=0, tiled=True),
-        lax.all_gather(w_colbert, "shard", axis=0, tiled=True),
-    )
-    query_w, query_b, key_w, value_w, value_b, out_w, out_b, gain_a, shift_a = attn_full
-    expand_w, expand_b, contract_w, contract_b, gain_b, shift_b, colbert_w = ffn_full
+    shards = lax.axis_size("shard")
+    part = width // shards
+    ff = b_expand.shape[0] * shards
+    small = jnp.stack(
+        [b_query, b_value, b_attn_out, gain_one, shift_one, b_contract, gain_two, shift_two]
+        + [b_expand[i * part : (i + 1) * part] for i in range(ff // width)]
+    )
+    small = lax.all_gather(small, "shard", axis=0)
+    query_b, value_b, out_b, gain_a, shift_a, contract_b, gain_b, shift_b = [
+        small[:, i].reshape(width) for i in range(8)
+    ]
+    expand_b = small[:, 8:].reshape(ff)
+    attn_w = gather_rows(jnp.concatenate([w_query, w_key, w_value], axis=1))
+    query_w, key_w, value_w = [attn_w[:, i * width : (i + 1) * width] for i in range(3)]
+    mid_w = gather_rows(jnp.concatenate([w_attn_out, w_expand, w_colbert], axis=1))
+    out_w, expand_w, colbert_w = (
+        mid_w[:, :width],
+        mid_w[:, width : width + ff],
+        mid_w[:, width + ff :],
+    )
+    contract_w = gather_rows(w_contract)
     inputs = tokens.reshape(row_count, width)
     positions = jnp.arange(seq_len, dtype=jnp.int32)
     valid_f = (positions[None, :] < lengths[:, None]).astype(jnp.float32).reshape(row_count, 1)
@@ -277,30 +290,6 @@
             jnp.sum(contracted * contracted * valid_f),
         ]
     )
-    sums, count = lax.psum((squares, jnp.sum(valid_f)), ("replica", "shard"))
-    rms_values = jnp.sqrt(sums / (count * width))
-    ffn_back = (
-        lax.all_gather(w_expand, "shard", axis=0, tiled=True),
-        lax.all_gather(b_expand, "shard", axis=0, tiled=True),
-        lax.all_gather(w_contract, "shard", axis=0, tiled=True),
-        lax.all_gather(b_contract, "shard", axis=0, tiled=True),
-        lax.all_gather(gain_two, "shard", axis=0, tiled=True),
-        lax.all_gather(shift_two, "shard", axis=0, tiled=True),
-        lax.all_gather(w_colbert, "shard", axis=0, tiled=True),
-    )
-    attn_back = (
-        lax.all_gather(w_query, "shard", axis=0, tiled=True),
-        lax.all_gather(b_query, "shard", axis=0, tiled=True),
-        lax.all_gather(w_key, "shard", axis=0, tiled=True),
-        lax.all_gather(w_value, "shard", axis=0, tiled=True),
-        lax.all_gather(b_value, "shard", axis=0, tiled=True),
-        lax.all_gather(w_attn_out, "shard", axis=0, tiled=True),
-        lax.all_gather(b_attn_out, "shard", axis=0, tiled=True),
-        lax.all_gather(gain_one, "shard", axis=0, tiled=True),
-        lax.all_gather(shift_one, "shard", axis=0, tiled=True),
-    )
-    query_w, query_b, key_w, value_w, value_b, out_w, out_b, gain_a, shift_a = attn_back
-    expand_w, expand_b, contract_w, contract_b, gain_b, shift_b, colbert_w = ffn_back
     grad_norm = cotangent.reshape(row_count, -1).astype(jnp.float32) * valid_f
     grad_projected = (
         inverse_len
@@ -319,15 +308,7 @@
     grad_expanded = gelu_back(grad_activated)[0].astype(jnp.bfloat16)
     grad_expand_b = jnp.sum(grad_expanded, axis=0, dtype=jnp.float32)
     grad_expand_w = product_left_t(hidden_low, grad_expanded)
-    ffn_grads = reduce_ffn(
-        grad_expand_w,
-        grad_expand_b,
-        grad_contract_w,
-        grad_contract_b,
-        grad_gain_two,
-        grad_shift_two,
-        grad_colbert,
-    )
+    r_wc = reduce_rows(grad_contract_w)
     grad_hidden_one = grad_sum_two + product_right_t(grad_expanded, expand_w)
     grad_sum_one, grad_gain_one, grad_shift_one = norm_backward(
         grad_hidden_one, gain_a, normed_one, inverse_one
@@ -335,6 +316,9 @@
     grad_attended = grad_sum_one.astype(jnp.bfloat16)
     grad_out_b = jnp.sum(grad_attended, axis=0, dtype=jnp.float32)
     grad_out_w = product_left_t(context, grad_attended)
+    r_mid = reduce_rows(
+        jnp.concatenate([grad_out_w, grad_expand_w, grad_colbert], axis=1)
+    )
     grad_context = product_right_t(grad_attended, out_w).astype(jnp.bfloat16)
     grad_queries, grad_keys, grad_values = lax.map(
         attend_backward,
@@ -355,17 +339,29 @@
     grad_query_w = product_left_t(inputs, grad_queries)
     grad_key_w = product_left_t(inputs, grad_keys)
     grad_value_w = product_left_t(inputs, grad_values)
-    attn_grads = reduce_attn(
-        grad_query_w,
-        grad_query_b,
-        grad_key_w,
-        grad_value_w,
-        grad_value_b,
-        grad_out_w,
-        grad_out_b,
-        grad_gain_one,
-        grad_shift_one,
-    )
+    r_attn = reduce_rows(jnp.concatenate([grad_query_w, grad_key_w, grad_value_w], axis=1))
+    sums = jnp.concatenate([squares, jnp.sum(valid_f)[None], jnp.zeros(width - 4, jnp.float32)])
+    vectors = jnp.stack(
+        [
+            grad_query_b,
+            grad_value_b,
+            grad_out_b,
+            grad_gain_one,
+            grad_shift_one,
+            grad_contract_b,
+            grad_gain_two,
+            grad_shift_two,
+            sums,
+        ]
+    )
+    vectors = jnp.concatenate([vectors, grad_expand_b.reshape(ff // width, width)])
+    vectors = sum_everywhere(vectors)
+    rms_values = jnp.sqrt(vectors[8, :3] / (vectors[8, 3] * width))
+    r_be = lax.dynamic_slice_in_dim(
+        vectors[9:].reshape(ff), lax.axis_index("shard") * (ff // shards), ff // shards
+    )
+    own = lax.dynamic_slice_in_dim(vectors, lax.axis_index("shard") * part, part, 1)
+    r_bq, r_bv, r_bo, r_ga, r_sa, r_bc, r_gb, r_sb = [own[i] for i in range(8)]
     grad_inputs = (
         grad_sum_one
         + product_right_t(grad_queries, query_w)
@@ -373,8 +369,12 @@
         + product_right_t(grad_values, value_w)
     )
     grad_tokens = grad_inputs.astype(jnp.bfloat16).reshape(seq_count, seq_len, width)
-    r_wq, r_bq, r_wk, r_wv, r_bv, r_wo, r_bo, r_ga, r_sa = attn_grads
-    r_we, r_be, r_wc, r_bc, r_gb, r_sb, r_wp = ffn_grads
+    r_wq, r_wk, r_wv = [r_attn[:, i * width : (i + 1) * width] for i in range(3)]
+    r_wo, r_we, r_wp = (
+        r_mid[:, :width],
+        r_mid[:, width : width + ff],
+        r_mid[:, width + ff :],
+    )
     return (
         embeddings,
         grad_tokens,

time: 1160 us -> 590 us (0.51)
  waiting for transfers between devices: 654 us -> 115 us
  blocking collectives: 161 us -> 45.8 us
  local copies, waits for them, and re-layouts: 67.9 us -> 121 us
  starting transfers between devices: 1.01 us -> 37.1 us
  other arithmetic: 63.3 us -> 78.3 us
  between operations: 17.6 us -> 2.63 us
    reduce_scatter x6 -> x0, waiting for transfers between devices: 454 us -> none  [the longest x1 88.7 us: reduce_attn(): lax.psum_scatter(regroup(g_wo), ('replica', 'shard'), scatter_dimension=0...]
    all_gather x8 -> x0, waiting for transfers between devices: 135 us -> none  [the longest x1 47.5 us: per_device(): lax.all_gather(w_expand, 'shard', axis=0, tiled=True)]
    ppermute x0 -> x44, waiting for transfers between devices: none -> 115 us  [the longest x6 55.2 us: reduce_rows(): other = lax.ppermute(low, 'replica', replica_partners(distance))]
    unnamed x3 -> x0, blocking collectives: 73 us -> none
    unnamed x16 -> x0, waiting for transfers between devices: 65.3 us -> none
    all_gather x7 -> x1, blocking collectives: 88 us -> 45.8 us  [per_device(): small = lax.all_gather(small, 'shard', axis=0)]
    ppermute x0 -> x44, starting transfers between devices: none -> 37.1 us  [the longest x9 10.5 us: reduce_rows(): lax.ppermute(sums[distance].astype(jnp.bfloat16), 'shard', shard_partners...]
    dynamic_update_slice x0 -> x21, local copies, waits for them, and re-layouts: none -> 25.7 us  [the longest x9 13.4 us: gather_rows(): full = lax.dynamic_update_slice_in_dim(full, near, start + core * half, 0)]
  transfers between devices with their start and end apart: 15 -> 44, of which waited for: 13 -> 13; matrix products, arithmetic and copies ran while one was open for 22% -> 30% of each run, Pallas kernels for 0% -> 0%
where the time goes in v1:
time: 590 us; the launch traced here: 580 us
  matrix products  180 us (31%)
  local copies, waits for them, and re-layouts  121 us (21%)
  waiting for transfers between devices  115 us (19%)
  other arithmetic  78.3 us (13%)
  blocking collectives  45.8 us (8%)
  starting transfers between devices  37.1 us (6%)
    dot_general x7, matrix products, product(): return jnp.dot(left, right, preferred_element_type=jnp.float32)  55.9 us
    ppermute x6, waiting for transfers between devices, reduce_rows(): other = lax.ppermute(low, 'replica', replica_partners(distance))  55.2 us
    dot_general x7, matrix products, product_right_t(): lax.dot_general(left, right, (((1,), (1,)), ((), ())), preferred_element_...  52.9 us
    all_gather x1, blocking collectives, per_device(): small = lax.all_gather(small, 'shard', axis=0)  45.8 us
    ppermute x9, waiting for transfers between devices, reduce_rows(): lax.ppermute(sums[distance].astype(jnp.bfloat16), 'shard', shard_partners...  36.9 us
    dot_general x7, matrix products, product_left_t(): lax.dot_general(left, right, (((0,), (0,)), ((), ())), preferred_element_...  27.3 us
    ppermute x9, waiting for transfers between devices, gather_rows(): near = lax.ppermute(sent, 'shard', shard_partners(distance))  20.7 us
    dynamic_slice x18, local copies, waits for them, and re-layouts, per_device(): lax.map(attend_sequence, (queries.reshape(seq_shape), keys_all.reshape(se...  15.5 us
  transfers between devices with their start and end apart: 44, of which 13 were waited for; matrix products, arithmetic and copies ran while one was open for 30% of the time, Pallas kernels for 0%

profile of v1, /device:TPU:0, one launch (start us, length us, event | category | flops | bytes accessed | tf_op | source)
XLA Modules:
  0.0 580.2 jit_solution(7713925663709086039)
XLA Ops:
  16.4 45.8 %all-gather.1 = bf16[4,12,192]{2,1,0:T(8,128)(2,1)S(1)} all-gather(bf16[1,12,192]{2,1,0:T(8,128)(2,1)S(1)} %bitcast.209), channel_id=2, replica_groups=mesh['replica'=8,'shard'=4] {'shard'}, dimensions={0}, use_global_device_ids=true | all-gather | bytes 23040 | tf_op jit(solution)/shard_map/all_gather | solution.py:242
  95.2 13.7 %collective-permute-done.2 = bf16[96,2304]{1,0:T(8,128)(2,1)S(1)} collective-permute-done((bf16[96,2304]{1,0:T(8,128)(2,1)}, bf16[96,2304]{1,0:T(8,128)(2,1)S(1)}, u32[]{:S(2)}, u32[]{:S(2)}) %collective-permute-start.2) | collective-permute-done | bytes 442400 | tf_op jit(solution)/shard_map/ppermute | solution.py:160
  122.1 7.0 %collective-permute-done.10 = bf16[96,3968]{1,0:T(8,128)(2,1)} collective-permute-done((bf16[96,3968]{1,0:T(8,128)(2,1)}, bf16[96,3968]{1,0:T(8,128)(2,1)}, u32[]{:S(2)}, u32[]{:S(2)}) %collective-permute-start.10) | collective-permute-done | bytes 761888 | tf_op jit(solution)/shard_map/ppermute | solution.py:160
  129.2 27.4 %while.10 = (s32[]{:T(128)}, bf16[2,512,768]{2,1,0:T(8,128)(2,1)}, f32[2,1,12,512]{3,2,1,0:T(8,128)}, bf16[2,512,768]{1,2,0:T(8,128)(2,1)S(1)}, s32[2]{0:T(128)S...) while((s32[]{:T(128)}, bf16[2,512,768]{2,1,0:T(8,128)(2,1)}, ...), condition=%wide.region_3.4_spmd, body=%wide.region_0.3_spmd.sunk | while | flops 843442688 | bytes 48965756 | solution.py:263
  178.6 36.7 %multiply_convert_fusion.3 = (bf16[1024,3072]{1,0:T(8,128)(2,1)S(1)}, f32[1024,3072]{1,0:T(8,128)}, f32[1024,3072]{1,0:T(8,128)}) fusion(f32[3072]{0:T(1024)S(1)} %copy-done.46, bf16[768,3968]{1,0:T(8,128)(2,1)} %constant_dynamic-update-slice_fusion.17, f32[1024,768]{1,0:T(8,128)S(1)} %get-tuple-element.336, f32[768]{0:T(1024)S(1)} %copy-done.52, ...), kind=kOutput, calls=%fused_computation.39 | convolution fusion | flops 5043388416 | bytes 39348224 | tf_op jit(solution)/shard_map/dot_general | solution.py:17
  215.3 9.0 %multiply_reduce_fusion.1 = (f32[]{:T(128)}, f32[]{:T(128)}, f32[1024]{0:T(1024)S(1)}, f32[1024,768]{1,0:T(8,128)S(1)}) fusion(f32[1024]{0:T(1024)S(1)} %bitcast.206, f32[768]{0:T(1024)S(1)} %copy-done.53, f32[1024,768]{1,0:T(8,128)S(1)} %get-tuple-element.393, f32[768]{0:T(1024)S(1)} %copy-done.44, f32[768]{0:T(1024)S(1)} %copy-done.52, ...), kind=kOutput, calls=%fused_computation.59 | convolution fusion | flops 4842847232 | bytes 20475912 | tf_op jit(solution)/shard_map/dot_general | solution.py:17
  234.8 7.1 %fusion.67 = bf16[3072,768]{1,0:T(8,128)(2,1)} fusion(bf16[1024,3072]{1,0:T(8,128)(2,1)S(1)} %get-tuple-element.333, f32[1024,768]{1,0:T(8,128)S(1)} %get-tuple-element.328), kind=kOutput, calls=%fused_computation.241 | convolution fusion | flops 4832624640 | bytes 14155776 | tf_op jit(solution)/shard_map/dot_general | solution.py:21
  241.9 19.4 %convert_reduce_fusion = (f32[3072]{0:T(1024)}, bf16[1024,3072]{1,0:T(8,128)(2,1)}) fusion(f32[1024,3072]{1,0:T(8,128)} %get-tuple-element.334, bf16[3072,768]{1,0:T(8,128)(2,1)} %constant_dynamic-update-slice_fusion.10, f32[1024,768]{1,0:T(8,128)} %copy-done.18, f32[1024,3072]{1,0:T(8,128)} %get-tuple-element.394, f32[3072]{0:T(1024)S(1)} %copy-done.46), kind=kOutput, calls=%fused_computation.37 | convolution fusion | flops 4886098944 | bytes 39346176 | tf_op jit(solution)/shard_map/dot_general | solution.py:27
  261.3 10.8 %multiply_reduce_fusion.5 = (f32[768]{0:T(1024)}, f32[1024]{0:T(1024)S(1)}, f32[1024]{0:T(1024)S(1)}, f32[768]{0:T(1024)}, f32[1024,768]{1,0:T(8,128)S(1)}) fusion(f32[1024,768]{1,0:T(8,128)S(1)} %get-tuple-element.336, f32[1024]{0:T(1024)S(1)} %add_rsqrt_fusion.2, f32[1024]{0:T(1024)S(1)} %broadcast_multiply_fusion.5, f32[768]{0:T(1024)S(1)} %copy-done.43, ...), kind=kOutput, calls=%fused_computation.64 | convolution fusion | flops 4839698432 | bytes 20472832 | tf_op jit(solution)/shard_map/dot_general | solution.py:27
  272.1 8.2 %fusion.70 = bf16[768,3072]{1,0:T(8,128)(2,1)} fusion(bf16[1024,3072]{1,0:T(8,128)(2,1)S(1)} %copy-done.67, f32[1024,768]{1,0:T(8,128)S(1)} %get-tuple-element.336, f32[768]{0:T(1024)S(1)} %copy-done.52, f32[768]{0:T(1024)S(1)} %copy-done.43, f32[1024]{0:T(1024)S(1)} %add_rsqrt_fusion.2, f32[1024]{0:T(1024)S(1)} %broadcast_multiply_fusion.5), kind=kOutput, calls=%fused_computation.244 | convolution fusion | flops 4835770368 | bytes 14170112 | tf_op jit(solution)/shard_map/dot_general | solution.py:21
  282.0 4.9 convolution_convert_fusion
  289.5 65.0 %while.27 = (s32[]{:T(128)}, bf16[2,512,768]{1,2,0:T(8,128)(2,1)}, bf16[2,512,768]{1,2,0:T(8,128)(2,1)}, bf16[2,512,768]{1,2,0:T(8,128)(2,1)}, bf16[2,512,768]{1...) while((s32[]{:T(128)}, bf16[2,512,768]{1,2,0:T(8,128)(2,1)}, ...), condition=%wide.region_16.17_spmd, body=%wide.region_14.16_spmd.sunk | while | flops 2062412288 | bytes 152742224 | solution.py:323
  301.1 7.4 %multiply_reduce_fusion.14 = (f32[12,512]{1,0:T(8,128)S(1)}, f32[12,512,512]{1,2,0:T(8,128)}) fusion(f32[12,512,512]{1,2,0:T(8,128)S(1)} %fusion.151, f32[12,512]{1,0:T(8,128)S(1)} %dynamic-slice_bitcast_fusion.2, pred[512]{0:T(512)(128)(4,1)S(1)} %iota_compare_fusion.5, bf16[512,12,64]{0,2,1:T(8,128)(2,1)S(1)} %bitcast.180, ...), kind=kOutput, calls=%fused_computation.16.clone.1 | convolution fusion | flops 418375680 | bytes 26788352 | tf_op jit(solution)/shard_map/while/body/eval_jaxpr/while/body/eval_jaxpr/qhd,khd->hqk/dot_general | solution.py:110
  308.5 7.1 %multiply_convert_fusion.8 = bf16[12,512,512]{1,2,0:T(8,128)(2,1)S(1)} fusion(f32[12,512,512]{1,2,0:T(8,128)} %get-tuple-element.519, f32[12,512,512]{1,2,0:T(8,128)S(1)} %fusion.151, f32[12,512]{1,0:T(8,128)S(1)} %get-tuple-element.520, f32[12,512]{1,0:T(8,128)S(1)} %dynamic-slice_bitcast_fusion.2, pred[512]{0:T(512)(128)(4,1)S(1)} %iota_compare_fusion.5), kind=kLoop, calls=%fused_computation.15.clone.1 | loop fusion | flops 18874368 | bytes 31506944 | tf_op jit(solution)/shard_map/while/body/eval_jaxpr/while/body/eval_jaxpr/convert_element_type | solution.py:116
  333.3 7.4 %multiply_reduce_fusion.14 = (f32[12,512]{1,0:T(8,128)S(1)}, f32[12,512,512]{1,2,0:T(8,128)}) fusion(f32[12,512,512]{1,2,0:T(8,128)S(1)} %fusion.151, f32[12,512]{1,0:T(8,128)S(1)} %dynamic-slice_bitcast_fusion.2, pred[512]{0:T(512)(128)(4,1)S(1)} %iota_compare_fusion.5, bf16[512,12,64]{0,2,1:T(8,128)(2,1)S(1)} %bitcast.180, ...), kind=kOutput, calls=%fused_computation.16.clone.1 | convolution fusion | flops 418375680 | bytes 26788352 | tf_op jit(solution)/shard_map/while/body/eval_jaxpr/while/body/eval_jaxpr/qhd,khd->hqk/dot_general | solution.py:110
  340.7 7.1 %multiply_convert_fusion.8 = bf16[12,512,512]{1,2,0:T(8,128)(2,1)S(1)} fusion(f32[12,512,512]{1,2,0:T(8,128)} %get-tuple-element.519, f32[12,512,512]{1,2,0:T(8,128)S(1)} %fusion.151, f32[12,512]{1,0:T(8,128)S(1)} %get-tuple-element.520, f32[12,512]{1,0:T(8,128)S(1)} %dynamic-slice_bitcast_fusion.2, pred[512]{0:T(512)(128)(4,1)S(1)} %iota_compare_fusion.5), kind=kLoop, calls=%fused_computation.15.clone.1 | loop fusion | flops 18874368 | bytes 31506944 | tf_op jit(solution)/shard_map/while/body/eval_jaxpr/while/body/eval_jaxpr/convert_element_type | solution.py:116
  404.3 4.9 fusion.35
  427.4 5.0 fusion.32
  457.1 11.1 %collective-permute-done.40 = bf16[384,768]{1,0:T(8,128)(2,1)} collective-permute-done((bf16[384,768]{1,0:T(8,128)(2,1)}, bf16[384,768]{1,0:T(8,128)(2,1)}, u32[]{:S(2)}, u32[]{:S(2)}) %collective-permute-start.40) | collective-permute-done | bytes 589856 | tf_op jit(solution)/shard_map/ppermute | solution.py:187
  469.9 5.0 add_convert_fusion.1
  484.8 13.8 %collective-permute-done.33 = bf16[96,3968]{1,0:T(8,128)(2,1)} collective-permute-done((bf16[96,3968]{1,0:T(8,128)(2,1)}, bf16[96,3968]{1,0:T(8,128)(2,1)}, u32[]{:S(2)}, u32[]{:S(2)}) %collective-permute-start.33) | collective-permute-done | bytes 761888 | tf_op jit(solution)/shard_map/ppermute | solution.py:187
  508.0 17.1 %collective-permute-done.34 = bf16[96,3968]{1,0:T(8,128)(2,1)} collective-permute-done((bf16[96,3968]{1,0:T(8,128)(2,1)S(1)}, bf16[96,3968]{1,0:T(8,128)(2,1)}, u32[]{:S(2)}, u32[]{:S(2)}) %collective-permute-start.34) | collective-permute-done | bytes 761888 | tf_op jit(solution)/shard_map/ppermute | solution.py:193
  529.2 23.2 %collective-permute-done.42 = bf16[384,768]{1,0:T(8,128)(2,1)S(1)} collective-permute-done((bf16[384,768]{1,0:T(8,128)(2,1)S(1)}, bf16[384,768]{1,0:T(8,128)(2,1)S(1)}, u32[]{:S(2)}, u32[]{:S(2)}) %collective-permute-start.42) | collective-permute-done | bytes 589856 | tf_op jit(solution)/shard_map/ppermute | solution.py:193
  553.3 15.0 %collective-permute-done.35 = bf16[96,3968]{1,0:T(8,128)(2,1)S(1)} collective-permute-done((bf16[96,3968]{1,0:T(8,128)(2,1)S(1)}, bf16[96,3968]{1,0:T(8,128)(2,1)S(1)}, u32[]{:S(2)}, u32[]{:S(2)}) %collective-permute-start.35) | collective-permute-done | bytes 761888 | tf_op jit(solution)/shard_map/ppermute | solution.py:193
  (457 shorter events, 290.0 us)
Async XLA Ops:
  2.7 109.6 %collective-permute-start.16 = (bf16[384,768]{1,0:T(8,128)(2,1)}, bf16[384,768]{1,0:T(8,128)(2,1)}, u32[]{:S(2)}, u32[]{:S(2)}) collective-permute-start(bf16[384,768]{1,0:T(8,128)(2,1)} %constant_dynamic-slice_fusion.8), channel_id=1, source_target_pairs={{0,3},{1,2},{2,1},{3,0},{4,7},{5,6},{6,5},{7,4},{8,11},{9,10},{10,... | collective-permute-start | bytes 1769480 | tf_op jit(solution)/shard_map/ppermute | solution.py:160
  6.6 106.2 %collective-permute-start.14 = (bf16[384,768]{1,0:T(8,128)(2,1)}, bf16[384,768]{1,0:T(8,128)(2,1)}, u32[]{:S(2)}, u32[]{:S(2)}) collective-permute-start(bf16[384,768]{1,0:T(8,128)(2,1)} %constant_dynamic-slice_fusion.8), channel_id=1, source_target_pairs={{0,2},{1,3},{2,0},{3,1},{4,6},{5,7},{6,4},{7,5},{8,10},{9,11},{10,... | collective-permute-start | bytes 1769480 | tf_op jit(solution)/shard_map/ppermute | solution.py:160
  7.1 83.5 %collective-permute-start.12 = (bf16[384,768]{1,0:T(8,128)(2,1)}, bf16[384,768]{1,0:T(8,128)(2,1)}, u32[]{:S(2)}, u32[]{:S(2)}) collective-permute-start(bf16[384,768]{1,0:T(8,128)(2,1)} %constant_dynamic-slice_fusion.8), channel_id=1, source_target_pairs={{0,1},{1,0},{2,3},{3,2},{4,5},{5,4},{6,7},{7,6},{8,9},{9,8},{10,11... | collective-permute-start | bytes 1769480 | tf_op jit(solution)/shard_map/ppermute | solution.py:160
  11.2 76.9 %collective-permute-start = (bf16[96,2304]{1,0:T(8,128)(2,1)}, bf16[96,2304]{1,0:T(8,128)(2,1)}, u32[]{:S(2)}, u32[]{:S(2)}) collective-permute-start(bf16[96,2304]{1,0:T(8,128)(2,1)} %constant_dynamic-slice_fusion.10), channel_id=1, source_target_pairs={{0,1},{1,0},{2,3},{3,2},{4,5},{5,4},{6,7},{7,6},{8,9},{9,8},{10,11... | collective-permute-start | bytes 1327112 | tf_op jit(solution)/shard_map/ppermute | solution.py:160
  15.4 77.7 %collective-permute-start.6 = (bf16[96,3968]{1,0:T(8,128)(2,1)}, bf16[96,3968]{1,0:T(8,128)(2,1)}, u32[]{:S(2)}, u32[]{:S(2)}) collective-permute-start(bf16[96,3968]{1,0:T(8,128)(2,1)} %constant_dynamic-slice_fusion.9), channel_id=1, source_target_pairs={{0,1},{1,0},{2,3},{3,2},{4,5},{5,4},{6,7},{7,6},{8,9},{9,8},{10,11... | collective-permute-start | bytes 2285576 | tf_op jit(solution)/shard_map/ppermute | solution.py:160
  88.1 22.3 %collective-permute-start.4 = (bf16[96,2304]{1,0:T(8,128)(2,1)}, bf16[96,2304]{1,0:T(8,128)(2,1)S(1)}, u32[]{:S(2)}, u32[]{:S(2)}) collective-permute-start(bf16[96,2304]{1,0:T(8,128)(2,1)} %constant_dynamic-slice_fusion.10), channel_id=1, source_target_pairs={{0,3},{1,2},{2,1},{3,0},{4,7},{5,6},{6,5},{7,4},{8,11},{9,10},{10,... | collective-permute-start | bytes 1327112 | tf_op jit(solution)/shard_map/ppermute | solution.py:160
  110.4 46.1 %collective-permute-start.8 = (bf16[96,3968]{1,0:T(8,128)(2,1)}, bf16[96,3968]{1,0:T(8,128)(2,1)}, u32[]{:S(2)}, u32[]{:S(2)}) collective-permute-start(bf16[96,3968]{1,0:T(8,128)(2,1)} %constant_dynamic-slice_fusion.9), channel_id=1, source_target_pairs={{0,2},{1,3},{2,0},{3,1},{4,6},{5,7},{6,4},{7,5},{8,10},{9,11},{10,... | collective-permute-start | bytes 2285576 | tf_op jit(solution)/shard_map/ppermute | solution.py:160
  112.4 44.7 %collective-permute-start.13 = (bf16[384,768]{1,0:T(8,128)(2,1)}, bf16[384,768]{1,0:T(8,128)(2,1)}, u32[]{:S(2)}, u32[]{:S(2)}) collective-permute-start(bf16[384,768]{1,0:T(8,128)(2,1)} %collective-permute-done.12), channel_id=1, source_target_pairs={{0,4},{4,0},{8,12},{12,8},{16,20},{20,16},{24,28},{28,24},{1,5},{5... | collective-permute-start | bytes 1769480 | tf_op jit(solution)/shard_map/ppermute | solution.py:161
  112.8 52.0 %collective-permute-start.17 = (bf16[384,768]{1,0:T(8,128)(2,1)}, bf16[384,768]{1,0:T(8,128)(2,1)}, u32[]{:S(2)}, u32[]{:S(2)}) collective-permute-start(bf16[384,768]{1,0:T(8,128)(2,1)} %collective-permute-done.16), channel_id=1, source_target_pairs={{0,4},{4,0},{8,12},{12,8},{16,20},{20,16},{24,28},{28,24},{1,5},{5... | collective-permute-start | bytes 1769480 | tf_op jit(solution)/shard_map/ppermute | solution.py:161
  113.9 47.0 %collective-permute-start.15 = (bf16[384,768]{1,0:T(8,128)(2,1)}, bf16[384,768]{1,0:T(8,128)(2,1)}, u32[]{:S(2)}, u32[]{:S(2)}) collective-permute-start(bf16[384,768]{1,0:T(8,128)(2,1)} %collective-permute-done.14), channel_id=1, source_target_pairs={{0,4},{4,0},{8,12},{12,8},{16,20},{20,16},{24,28},{28,24},{1,5},{5... | collective-permute-start | bytes 1769480 | tf_op jit(solution)/shard_map/ppermute | solution.py:161
  129.2 37.6 %collective-permute-start.7 = (bf16[96,3968]{1,0:T(8,128)(2,1)}, bf16[96,3968]{1,0:T(8,128)(2,1)}, u32[]{:S(2)}, u32[]{:S(2)}) collective-permute-start(bf16[96,3968]{1,0:T(8,128)(2,1)} %collective-permute-done.6), channel_id=1, source_target_pairs={{0,4},{4,0},{8,12},{12,8},{16,20},{20,16},{24,28},{28,24},{1,5},{5... | collective-permute-start | bytes 2285576 | tf_op jit(solution)/shard_map/ppermute | solution.py:161
  373.9 61.9 %collective-permute-start.37 = (bf16[1536,768]{1,0:T(8,128)(2,1)}, bf16[1536,768]{1,0:T(8,128)(2,1)}, u32[]{:S(2)}, u32[]{:S(2)}) collective-permute-start(bf16[1536,768]{1,0:T(8,128)(2,1)} %pad_maximum_fusion.3), channel_id=1, source_target_pairs={{0,4},{4,0},{8,12},{12,8},{16,20},{20,16},{24,28},{28,24},{1,5},{5... | collective-permute-start | bytes 7077896 | tf_op jit(solution)/shard_map/ppermute | solution.py:179
  382.4 64.6 %collective-permute-start.30 = (bf16[384,3968]{1,0:T(8,128)(2,1)}, bf16[384,3968]{1,0:T(8,128)(2,1)}, u32[]{:S(2)}, u32[]{:S(2)}) collective-permute-start(bf16[384,3968]{1,0:T(8,128)(2,1)} %pad_maximum_fusion.2), channel_id=1, source_target_pairs={{0,4},{4,0},{8,12},{12,8},{16,20},{20,16},{24,28},{28,24},{1,5},{5... | collective-permute-start | bytes 9142280 | tf_op jit(solution)/shard_map/ppermute | solution.py:179
  397.2 22.8 %collective-permute-start.19 = (bf16[96,2304]{1,0:T(8,128)(2,1)}, bf16[96,2304]{1,0:T(8,128)(2,1)}, u32[]{:S(2)}, u32[]{:S(2)}) collective-permute-start(bf16[96,2304]{1,0:T(8,128)(2,1)} %copy.89), channel_id=1, source_target_pairs={{0,1},{1,0},{2,3},{3,2},{4,5},{5,4},{6,7},{7,6},{8,9},{9,8},{10,11... | collective-permute-start | bytes 1327112 | tf_op jit(solution)/shard_map/ppermute | solution.py:187
  439.6 28.5 %collective-permute-start.40 = (bf16[384,768]{1,0:T(8,128)(2,1)}, bf16[384,768]{1,0:T(8,128)(2,1)}, u32[]{:S(2)}, u32[]{:S(2)}) collective-permute-start(bf16[384,768]{1,0:T(8,128)(2,1)} %get-tuple-element.349), channel_id=1, source_target_pairs={{0,3},{1,2},{2,1},{3,0},{4,7},{5,6},{6,5},{7,4},{8,11},{9,10},{10,... | collective-permute-start | bytes 1769480 | tf_op jit(solution)/shard_map/ppermute | solution.py:187
  440.9 36.7 %collective-permute-start.39 = (bf16[384,768]{1,0:T(8,128)(2,1)}, bf16[384,768]{1,0:T(8,128)(2,1)}, u32[]{:S(2)}, u32[]{:S(2)}) collective-permute-start(bf16[384,768]{1,0:T(8,128)(2,1)} %get-tuple-element.350), channel_id=1, source_target_pairs={{0,2},{1,3},{2,0},{3,1},{4,6},{5,7},{6,4},{7,5},{8,10},{9,11},{10,... | collective-permute-start | bytes 1769480 | tf_op jit(solution)/shard_map/ppermute | solution.py:187
  447.0 34.4 %collective-permute-start.23 = (bf16[96,2304]{1,0:T(8,128)(2,1)}, bf16[96,2304]{1,0:T(8,128)(2,1)}, u32[]{:S(2)}, u32[]{:S(2)}) collective-permute-start(bf16[96,2304]{1,0:T(8,128)(2,1)} %copy.97), channel_id=1, source_target_pairs={{0,16},{4,20},{8,24},{12,28},{16,0},{20,4},{24,8},{28,12},{1,17},{... | collective-permute-start | bytes 1327112 | tf_op jit(solution)/shard_map/ppermute | solution.py:193
  451.4 33.4 %collective-permute-start.31 = (bf16[96,3968]{1,0:T(8,128)(2,1)}, bf16[96,3968]{1,0:T(8,128)(2,1)}, u32[]{:S(2)}, u32[]{:S(2)}) collective-permute-start(bf16[96,3968]{1,0:T(8,128)(2,1)} %get-tuple-element.345), channel_id=1, source_target_pairs={{0,1},{1,0},{2,3},{3,2},{4,5},{5,4},{6,7},{7,6},{8,9},{9,8},{10,11... | collective-permute-start | bytes 2285576 | tf_op jit(solution)/shard_map/ppermute | solution.py:187
  455.8 42.8 %collective-permute-start.33 = (bf16[96,3968]{1,0:T(8,128)(2,1)}, bf16[96,3968]{1,0:T(8,128)(2,1)}, u32[]{:S(2)}, u32[]{:S(2)}) collective-permute-start(bf16[96,3968]{1,0:T(8,128)(2,1)} %get-tuple-element.346), channel_id=1, source_target_pairs={{0,3},{1,2},{2,1},{3,0},{4,7},{5,6},{6,5},{7,4},{8,11},{9,10},{10,... | collective-permute-start | bytes 2285576 | tf_op jit(solution)/shard_map/ppermute | solution.py:187
  468.1 31.7 %collective-permute-start.32 = (bf16[96,3968]{1,0:T(8,128)(2,1)S(1)}, bf16[96,3968]{1,0:T(8,128)(2,1)}, u32[]{:S(2)}, u32[]{:S(2)}) collective-permute-start(bf16[96,3968]{1,0:T(8,128)(2,1)S(1)} %get-tuple-element.347), channel_id=1, source_target_pairs={{0,2},{1,3},{2,0},{3,1},{4,6},{5,7},{6,4},{7,5},{8,10},{9,11},{10,... | collective-permute-start | bytes 2285576 | tf_op jit(solution)/shard_map/ppermute | solution.py:187
  479.7 25.3 %collective-permute-start.41 = (bf16[384,768]{1,0:T(8,128)(2,1)S(1)}, bf16[384,768]{1,0:T(8,128)(2,1)}, u32[]{:S(2)}, u32[]{:S(2)}) collective-permute-start(bf16[384,768]{1,0:T(8,128)(2,1)S(1)} %add_convert_fusion.13), channel_id=1, source_target_pairs={{0,8},{4,12},{8,0},{12,4},{16,24},{20,28},{24,16},{28,20},{1,9},{5... | collective-permute-start | bytes 1769480 | tf_op jit(solution)/shard_map/ppermute | solution.py:193
  502.4 22.7 %collective-permute-start.34 = (bf16[96,3968]{1,0:T(8,128)(2,1)S(1)}, bf16[96,3968]{1,0:T(8,128)(2,1)}, u32[]{:S(2)}, u32[]{:S(2)}) collective-permute-start(bf16[96,3968]{1,0:T(8,128)(2,1)S(1)} %add_convert_fusion.7), channel_id=1, source_target_pairs={{0,8},{4,12},{8,0},{12,4},{16,24},{20,28},{24,16},{28,20},{1,9},{5... | collective-permute-start | bytes 2285576 | tf_op jit(solution)/shard_map/ppermute | solution.py:193
  506.2 46.1 %collective-permute-start.42 = (bf16[384,768]{1,0:T(8,128)(2,1)S(1)}, bf16[384,768]{1,0:T(8,128)(2,1)S(1)}, u32[]{:S(2)}, u32[]{:S(2)}) collective-permute-start(bf16[384,768]{1,0:T(8,128)(2,1)S(1)} %add_convert_fusion.12), channel_id=1, source_target_pairs={{0,16},{4,20},{8,24},{12,28},{16,0},{20,4},{24,8},{28,12},{1,17},{... | collective-permute-start | bytes 1769480 | tf_op jit(solution)/shard_map/ppermute | solution.py:193
  526.3 41.9 %collective-permute-start.35 = (bf16[96,3968]{1,0:T(8,128)(2,1)S(1)}, bf16[96,3968]{1,0:T(8,128)(2,1)S(1)}, u32[]{:S(2)}, u32[]{:S(2)}) collective-permute-start(bf16[96,3968]{1,0:T(8,128)(2,1)S(1)} %add_convert_fusion.6), channel_id=1, source_target_pairs={{0,16},{4,20},{8,24},{12,28},{16,0},{20,4},{24,8},{28,12},{1,17},{... | collective-permute-start | bytes 2285576 | tf_op jit(solution)/shard_map/ppermute | solution.py:193
  (98 other events, 776.3 us)
